TPU v7x, 256 devices: a whole 4x4x8 slice. The times are simulated.
256 devices in a mesh: clus: 4 (over z_lo, core), sub: 64 (over x, z_hi, y).
Axes of the slice: x: 4, y: 4, z: 8 (z_hi: 4, z_lo: 2; z = z_hi * 2 + z_lo), core: 2. Of those that a mesh axis runs over, the one named last changes fastest.
Arguments:
- load: float32 [4, 64, 6, 256, 128], P('clus', 'sub'), may hold values from -30 to 30
- dual_op: float32 [4, 64, 1536, 1536], P('clus', 'sub'), may hold values from -6 to 17, as said below
- modes: float32 [4, 64, 32, 1536], P('clus', 'sub'), may hold values from -1 to 1
- face_map: int32 [4, 64, 3, 256], P('clus', 'sub'), may hold values from 0 to 255, each once within a row
- cluster: int32 [4, 64], P('clus', 'sub'), may hold values from 0 to 1, as said below
Outputs:
- multipliers: float32 [4, 64, 6, 256, 128], P('clus', 'sub')
- residual: float32 [4, 64, 6, 256, 128], P('clus', 'sub')
Inputs may be any that keep to these rules, and one draw needn't show every extreme that they name: `dual_op`: each subdomain's block is symmetric positive definite. `face_map`: each row of 256 entries names every row of the neighbour's face once. In every cluster group exactly half of the 64 subdomains belong to each of its two clusters.
All inputs are finite; a program needn't handle non-finite values.
Results may differ from a plain program's by a relative error of at most 0.00011.
Values sent between devices are 32-bit elements; how exact they have to be, the bound alone decides.
No kernel may reach another device: no remote copies, remote signals or barrier semaphores. Data moves between devices by JAX's collectives and lax.ppermute only.
A program may use at most 128 MiB of HBM per device.

v0:
```python
import jax
import jax.numpy as jnp
from jax import lax
from jax.sharding import PartitionSpec as P

FACE = 256
COLS = 128
ITERS = 3
ORDER = 1536
damping_factor = 0.8
highest = lax.Precision.HIGHEST


def with_halo(cells, sides, width):
    for axis, dim in sides:
        count = lax.axis_size(axis)
        head = lax.slice_in_dim(cells, 0, width, axis=dim)
        tail = lax.slice_in_dim(cells, cells.shape[dim] - width, cells.shape[dim], axis=dim)
        cells = jnp.concatenate(
            [
                lax.ppermute(tail, axis, [(i, (i + 1) % count) for i in range(count)]),
                cells,
                lax.ppermute(head, axis, [((i + 1) % count, i) for i in range(count)]),
            ],
            axis=dim,
        )
    return cells


def from_partner(array, axis, distance):
    return lax.ppermute(array, axis, [(i, i ^ 1 << distance) for i in range(lax.axis_size(axis))])


def partner_values(values, pairing, inverse):
    result = []
    for direction in range(3):
        plus_face = values[2 * direction]
        minus_face = values[2 * direction + 1]
        upward = jnp.take(plus_face, inverse[direction], axis=0)
        width = upward.shape[0]
        if direction == 0:
            arrived = with_halo(jnp.concatenate([minus_face, upward], axis=0), (("sub", 0),), width)
            from_minus = arrived[:width]
            from_plus = arrived[3 * width :]
        elif direction == 1:
            arrived = with_halo(
                jnp.concatenate([minus_face, upward], axis=0), (("clus", 0),), width
            )
            from_minus = arrived[:width]
            from_plus = arrived[3 * width :]
        else:
            bit_index = lax.axis_size("sub").bit_length() - 2
            arrived = from_partner(jnp.stack([upward, minus_face]), "sub", bit_index)
            from_minus = arrived[0]
            from_plus = arrived[1]
        plus_side = jnp.take(from_plus, pairing[direction], axis=0)
        result += [plus_side, from_minus]
    return jnp.stack(result)


def solve_one(lower_part, column_block):
    return jax.scipy.linalg.cho_solve((lower_part, True), column_block)


def per_device(load, dual_op, modes, face_map, cluster):
    values = load[0, 0]
    operator = dual_op[0, 0]
    mode_rows = modes[0, 0]
    pairing = face_map[0, 0]
    member = cluster[0, 0]
    inverse = jnp.argsort(pairing, axis=-1)
    plus_owned = pairing % 2 == 0
    minus_owned = jnp.broadcast_to(jnp.arange(FACE) % 2 == 1, plus_owned.shape)
    owned = jnp.stack([plus_owned, minus_owned], axis=1).reshape(6, FACE, 1).astype(jnp.float32)
    selector = (jnp.arange(2) == member).astype(jnp.float32)
    weighted = mode_rows * owned.reshape(1, ORDER)
    gram_terms = jnp.einsum("mn,kn->mk", weighted, mode_rows, precision=highest)
    gram_total = lax.psum(selector[:, None, None] * gram_terms[None], "sub")
    factor = jnp.linalg.cholesky(gram_total)
    residual = values * owned
    multipliers = jnp.zeros_like(values)
    for iteration in range(ITERS):
        projected = jnp.einsum(
            "mn,nc->mc", mode_rows, residual.reshape(ORDER, COLS), precision=highest
        )
        gathered = lax.psum(selector[:, None, None] * projected[None], "sub")
        coefficients = jax.vmap(solve_one)(factor, gathered)
        own_coeff = lax.dynamic_index_in_dim(coefficients, member, 0, keepdims=False)
        correction = jnp.einsum("mn,mc->nc", mode_rows, own_coeff, precision=highest).reshape(
            6, FACE, COLS
        )
        search = residual - owned * correction
        local_copy = search - (1.0 - owned) * partner_values(search, pairing, inverse)
        applied = jnp.dot(operator, local_copy.reshape(ORDER, COLS), precision=highest).reshape(
            6, FACE, COLS
        )
        assembled = owned * (applied - partner_values(applied, pairing, inverse))
        numerator, denominator = lax.psum(
            (jnp.sum(residual * search, axis=(0, 1)), jnp.sum(search * assembled, axis=(0, 1))),
            ("clus", "sub"),
        )
        step_size = damping_factor * numerator / denominator
        multipliers = multipliers + step_size * search
        residual = residual - step_size * assembled
    return (multipliers[None, None], residual[None, None])


def solution(mesh):
    placed = (
        P("clus", "sub", None, None, None),
        P("clus", "sub", None, None),
        P("clus", "sub", None, None),
        P("clus", "sub", None, None),
        P("clus", "sub"),
    )
    return jax.shard_map(
        per_device,
        mesh=mesh,
        in_specs=placed,
        out_specs=(P("clus", "sub", None, None, None), P("clus", "sub", None, None, None)),
        check_vma=False,
    )
```

profile of v0, /device:TPU:1, one launch (start us, length us, event | category | flops | bytes accessed | tf_op | source)
XLA Modules:
  0.0 1692.0 jit_solution(10219532640262902524)
XLA Ops:
  22.2 326.7 %all-reduce.3 = (f32[2,32,128]{2,1,0:T(8,128)S(1)}, f32[2,32,32]{1,2,0:T(8,128)S(1)}) all-reduce(f32[2,32,128]{2,1,0:T(8,128)S(1)} %broadcast_multiply_fusion.3, f32[2,32,32]{1,2,0:T(8,128)S(1)} %broadcast_multiply_fusion.4), channel_id=1, replica_groups=mesh['clus'=4,'sub'=64] {'sub'}, use_global_device_ids=true, to_apply=%region_3.4 | all-reduce | flops 10240 | bytes 81920 | tf_op jit(solution)/shard_map/psum | solution.py:86
  349.0 5.9 custom-call.9
  355.1 4.9 custom-call.12
  360.4 1.8 convolution_bitcast_fusion.2
  363.6 2.1 multiply_subtract_fusion.9
  366.9 1.9 slice_bitcast_fusion.19
  373.3 56.8 %collective-permute-start.3 = (f32[256,128]{0,1:T(8,128)}, f32[256,128]{0,1:T(8,128)}, u32[]{:S(2)}, u32[]{:S(2)}) collective-permute-start(f32[256,128]{0,1:T(8,128)} %broadcast_select_fusion.10), channel_id=1, source_target_pairs={{0,64},{64,128},{128,192},{192,0},{1,65},{65,129},{129,193},{193,1... | collective-permute-start | bytes 393224 | tf_op jit(solution)/shard_map/ppermute | solution.py:21
  430.1 8.1 collective-permute-start
  439.5 3.8 collective-permute-done
  445.8 1.6 bitcast_dynamic-update-slice_fusion.46
  448.0 1.6 bitcast_dynamic-update-slice_fusion.44
  454.5 12.2 fusion.6
  472.0 8.7 collective-permute-start.5
  487.9 7.4 collective-permute-done.6
  497.9 1.6 multiply_reduce_fusion.5
  500.7 77.2 %all-reduce.2 = (f32[128]{0:T(128)S(1)}, f32[128]{0:T(128)S(1)}) all-reduce(f32[128]{0:T(128)S(1)} %get-tuple-element.13, f32[128]{0:T(128)S(1)} %get-tuple-element.12), channel_id=1, replica_groups=mesh['clus'=4,'sub'=64] {'clus','sub'}, use_global_device_ids=true, to_apply=%region_8.11 | all-reduce | flops 256 | bytes 2048 | tf_op jit(solution)/shard_map/psum | solution.py:98
  581.6 316.0 %psum.74 = f32[2,32,128]{2,1,0:T(8,128)S(1)} all-reduce(f32[2,32,128]{2,1,0:T(8,128)S(1)} %broadcast_multiply_fusion.2), channel_id=1, replica_groups=mesh['clus'=4,'sub'=64] {'sub'}, use_global_device_ids=true, to_apply=%region_9.12 | all-reduce | flops 8192 | bytes 65536 | tf_op jit(solution)/shard_map/psum | solution.py:86
  900.0 2.3 copy.260
  902.3 2.6 multiply_subtract_fusion.6
  913.0 56.4 %collective-permute-start.12 = (f32[256,128]{0,1:T(8,128)}, f32[256,128]{0,1:T(8,128)S(1)}, u32[]{:S(2)}, u32[]{:S(2)}) collective-permute-start(f32[256,128]{0,1:T(8,128)} %get-tuple-element.53), channel_id=1, source_target_pairs={{64,0},{128,64},{192,128},{0,192},{65,1},{129,65},{193,129},{1,193... | collective-permute-start | bytes 393224 | tf_op jit(solution)/shard_map/ppermute | solution.py:23
  970.8 2.3 copy.292
  974.5 2.5 collective-permute-start.13
  977.0 1.6 pad_maximum_fusion.2
  982.3 2.4 collective-permute-done.11
  989.9 1.6 slice_dynamic-update-slice_fusion.1
  994.1 12.1 fusion.9
  1011.5 1.6 collective-permute-start.17
  1013.1 4.6 collective-permute-start.15
  1021.1 1.9 collective-permute-start.18
  1023.0 1.6 pad_maximum_fusion.3
  1029.9 1.9 collective-permute-done.16
  1034.4 1.6 slice_bitcast_fusion.8
  1042.0 2.3 copy.294
  1044.3 1.9 multiply_reduce_fusion.3
  1046.2 77.9 %all-reduce.1 = (f32[128]{0:T(128)S(1)}, f32[128]{0:T(128)S(1)}) all-reduce(f32[128]{0:T(128)S(1)} %get-tuple-element.17, f32[128]{0:T(128)S(1)} %get-tuple-element.16), channel_id=1, replica_groups=mesh['clus'=4,'sub'=64] {'clus','sub'}, use_global_device_ids=true, to_apply=%region_13.16 | all-reduce | flops 256 | bytes 2048 | tf_op jit(solution)/shard_map/psum | solution.py:98
  1128.3 316.1 %psum.77 = f32[2,32,128]{2,1,0:T(8,128)S(1)} all-reduce(f32[2,32,128]{2,1,0:T(8,128)S(1)} %broadcast_multiply_fusion.1), channel_id=1, replica_groups=mesh['clus'=4,'sub'=64] {'sub'}, use_global_device_ids=true, to_apply=%region_14.17 | all-reduce | flops 8192 | bytes 65536 | tf_op jit(solution)/shard_map/psum | solution.py:86
  1448.0 2.8 multiply_subtract_fusion.2
  1456.7 56.1 %collective-permute-start.22 = (f32[256,128]{0,1:T(8,128)}, f32[256,128]{0,1:T(8,128)S(1)}, u32[]{:S(2)}, u32[]{:S(2)}) collective-permute-start(f32[256,128]{0,1:T(8,128)} %get-tuple-element.41), channel_id=1, source_target_pairs={{64,0},{128,64},{192,128},{0,192},{65,1},{129,65},{193,129},{1,193... | collective-permute-start | bytes 393224 | tf_op jit(solution)/shard_map/ppermute | solution.py:23
  1514.0 2.3 copy.329
  1517.8 2.3 collective-permute-start.23
  1524.1 3.9 collective-permute-done.21
  1528.0 1.6 bitcast_dynamic-update-slice_fusion.20
  1530.2 1.6 bitcast_dynamic-update-slice_fusion.18
  1536.6 12.4 fusion.12
  1555.6 3.3 collective-permute-start.25
  1560.5 3.7 collective-permute-start.28
  1564.2 1.7 pad_maximum_fusion.5
  1570.3 1.8 bitcast_dynamic-update-slice_fusion.5
  1575.1 1.6 bitcast_dynamic-update-slice_fusion.10
  1576.7 1.6 bitcast_dynamic-update-slice_fusion.26
  1578.3 1.6 bitcast_dynamic-update-slice_fusion.4
  1579.8 1.7 bitcast_dynamic-update-slice_fusion.3
  1581.5 1.6 bitcast_dynamic-update-slice_fusion.15
  1584.4 1.6 bitcast_dynamic-update-slice_fusion.13
  1586.0 1.6 bitcast_dynamic-update-slice_fusion.2
  1587.6 1.6 bitcast_dynamic-update-slice_fusion.8
  1589.1 1.6 bitcast_dynamic-update-slice_fusion.24
  1593.8 1.6 slice_dynamic-update-slice_fusion.3
  1595.4 1.9 multiply_reduce_fusion.1
  1597.3 76.0 %all-reduce = (f32[128]{0:T(128)S(1)}, f32[128]{0:T(128)S(1)}) all-reduce(f32[128]{0:T(128)S(1)} %get-tuple-element.15, f32[128]{0:T(128)S(1)} %get-tuple-element.14), channel_id=1, replica_groups=mesh['clus'=4,'sub'=64] {'clus','sub'}, use_global_device_ids=true, to_apply=%region_18.21 | all-reduce | flops 256 | bytes 2048 | tf_op jit(solution)/shard_map/psum | solution.py:98
  1673.2 1.7 bitcast_dynamic-update-slice_fusion.1
  1674.9 1.6 bitcast_dynamic-update-slice_fusion
  1676.5 1.6 bitcast_dynamic-update-slice_fusion.6
  1678.7 3.7 multiply_subtract_fusion
  (387 shorter events, 146.5 us)
Async XLA Ops:
  7.2 8.6 sort.19.cloned.1.call-start
  12.9 473.6 %copy-start.20 = (s32[1024]{0:T(1024)}, s32[1024]{0:T(1024)S(1)}, u32[]{:S(2)}) copy-start(s32[1024]{0:T(1024)S(1)} %pad_clamp_fusion.5) | copy-start | bytes 12292
  12.9 347.4 %copy-start.41 = (f32[2]{0:T(128)}, f32[2]{0:T(128)S(1)}, u32[]{:S(2)}) copy-start(f32[2]{0:T(128)S(1)} %compare_convert_fusion) | copy-start | bytes 28
  15.7 438.8 %copy-start.1 = (f32[1536,128]{0,1:T(8,128)}, f32[1536,128]{0,1:T(8,128)S(1)}, u32[]{:S(2)}) copy-start(f32[1536,128]{0,1:T(8,128)S(1)} %copy.224) | copy-start | bytes 2359300
  18.3 451.4 %copy-start.22 = (s32[1024]{0:T(1024)}, s32[1024]{0:T(1024)S(1)}, u32[]{:S(2)}) copy-start(s32[1024]{0:T(1024)S(1)} %pad_clamp_fusion.4) | copy-start | bytes 12292
  19.2 352.7 %copy-start.23 = (pred[256]{0:T(512)(128)(4,1)S(1)}, pred[256]{0:T(512)(128)(4,1)}, u32[]{:S(2)}) copy-start(pred[256]{0:T(512)(128)(4,1)} %get-tuple-element.87) | copy-start | bytes 772
  19.2 353.4 %copy-start.26 = (pred[256]{0:T(512)(128)(4,1)S(1)}, pred[256]{0:T(512)(128)(4,1)}, u32[]{:S(2)}) copy-start(pred[256]{0:T(512)(128)(4,1)} %get-tuple-element.86) | copy-start | bytes 772
  19.3 418.9 %copy-start.29 = (pred[256]{0:T(512)(128)(4,1)S(1)}, pred[256]{0:T(512)(128)(4,1)}, u32[]{:S(2)}) copy-start(pred[256]{0:T(512)(128)(4,1)} %get-tuple-element.85) | copy-start | bytes 772
  362.2 82.9 %copy-start.38 = (pred[256]{0:T(512)(128)(4,1)S(1)}, pred[256]{0:T(512)(128)(4,1)}, u32[]{:S(2)}) copy-start(pred[256]{0:T(512)(128)(4,1)} %compare_and_fusion.5) | copy-start | bytes 772
  362.2 85.2 %copy-start.35 = (pred[256]{0:T(512)(128)(4,1)S(1)}, pred[256]{0:T(512)(128)(4,1)}, u32[]{:S(2)}) copy-start(pred[256]{0:T(512)(128)(4,1)} %compare_and_fusion.3) | copy-start | bytes 772
  363.6 86.9 %copy-start.32 = (pred[256]{0:T(512)(128)(4,1)S(1)}, pred[256]{0:T(512)(128)(4,1)}, u32[]{:S(2)}) copy-start(pred[256]{0:T(512)(128)(4,1)} %compare_and_fusion) | copy-start | bytes 772
  372.6 73.2 %collective-permute-start.1 = (f32[256,128]{0,1:T(8,128)}, f32[256,128]{0,1:T(8,128)}, u32[]{:S(2)}, u32[]{:S(2)}) collective-permute-start(f32[256,128]{0,1:T(8,128)} %broadcast_select_fusion.11), channel_id=1, source_target_pairs={{0,1},{1,2},{2,3},{3,4},{4,5},{5,6},{6,7},{7,8},{8,9},{9,10},{10,1... | collective-permute-start | bytes 393224 | tf_op jit(solution)/shard_map/ppermute | solution.py:21
  373.3 74.7 %collective-permute-start.3 = (f32[256,128]{0,1:T(8,128)}, f32[256,128]{0,1:T(8,128)}, u32[]{:S(2)}, u32[]{:S(2)}) collective-permute-start(f32[256,128]{0,1:T(8,128)} %broadcast_select_fusion.10), channel_id=1, source_target_pairs={{0,64},{64,128},{128,192},{192,0},{1,65},{65,129},{129,193},{193,1... | collective-permute-start | bytes 393224 | tf_op jit(solution)/shard_map/ppermute | solution.py:21
  430.1 8.4 collective-permute-start.2
  430.1 13.2 collective-permute-start
  438.2 11.4 collective-permute-start.4
  451.9 15.9 copy-start.30
  453.3 15.6 copy-start.27
  454.5 26.3 %copy-start.24 = (pred[256]{0:T(512)(128)(4,1)S(1)}, pred[256]{0:T(512)(128)(4,1)}, u32[]{:S(2)}) copy-start(pred[256]{0:T(512)(128)(4,1)} %get-tuple-element.87) | copy-start | bytes 772
  470.5 14.9 collective-permute-start.7
  472.0 14.3 collective-permute-start.5
  482.8 97.2 %copy-start = (f32[1,1,32,1536]{3,2,1,0:T(8,128)S(1)}, f32[1,1,32,1536]{3,2,1,0:T(8,128)}, u32[]{:S(2)}) copy-start(f32[1,1,32,1536]{3,2,1,0:T(8,128)} %param.11) | copy-start | bytes 589828
  484.0 11.3 collective-permute-start.6
  484.0 12.0 collective-permute-start.8
  485.4 10.6 collective-permute-start.9
  486.3 9.8 copy-start.10
  487.3 8.7 copy-start.12
  497.0 407.9 %copy-start.8 = (f32[256,128]{0,1:T(8,128)}, f32[256,128]{0,1:T(8,128)S(1)}, u32[]{:S(2)}) copy-start(f32[256,128]{0,1:T(8,128)S(1)} %copy.251) | copy-start | bytes 393220
  898.8 81.0 %copy-start.21 = (s32[1024]{0:T(1024)S(1)}, s32[1024]{0:T(1024)}, u32[]{:S(2)}) copy-start(s32[1024]{0:T(1024)} %copy-done.20) | copy-start | bytes 12292
  900.0 81.4 %copy-start.39 = (pred[256]{0:T(512)(128)(4,1)S(1)}, pred[256]{0:T(512)(128)(4,1)}, u32[]{:S(2)}) copy-start(pred[256]{0:T(512)(128)(4,1)} %compare_and_fusion.5) | copy-start | bytes 772
  902.3 83.3 %copy-start.36 = (pred[256]{0:T(512)(128)(4,1)S(1)}, pred[256]{0:T(512)(128)(4,1)}, u32[]{:S(2)}) copy-start(pred[256]{0:T(512)(128)(4,1)} %compare_and_fusion.3) | copy-start | bytes 772
  902.3 87.0 %copy-start.33 = (pred[256]{0:T(512)(128)(4,1)S(1)}, pred[256]{0:T(512)(128)(4,1)}, u32[]{:S(2)}) copy-start(pred[256]{0:T(512)(128)(4,1)} %compare_and_fusion) | copy-start | bytes 772
  906.0 88.1 %copy-start.4 = (f32[1536,128]{0,1:T(8,128)S(1)}, f32[1536,128]{0,1:T(8,128)}, u32[]{:S(2)}) copy-start(f32[1536,128]{0,1:T(8,128)} %copy-done.3) | copy-start | bytes 2359300
  913.0 65.8 %collective-permute-start.12 = (f32[256,128]{0,1:T(8,128)}, f32[256,128]{0,1:T(8,128)S(1)}, u32[]{:S(2)}, u32[]{:S(2)}) collective-permute-start(f32[256,128]{0,1:T(8,128)} %get-tuple-element.53), channel_id=1, source_target_pairs={{64,0},{128,64},{192,128},{0,192},{65,1},{129,65},{193,129},{1,193... | collective-permute-start | bytes 393224 | tf_op jit(solution)/shard_map/ppermute | solution.py:23
  969.5 10.3 collective-permute-start.10
  973.0 11.6 collective-permute-start.11
  974.5 11.1 collective-permute-start.13
  978.6 8.6 collective-permute-start.14
  991.5 16.6 copy-start.31
  992.9 16.9 copy-start.28
  994.1 23.7 %copy-start.25 = (pred[256]{0:T(512)(128)(4,1)S(1)}, pred[256]{0:T(512)(128)(4,1)}, u32[]{:S(2)}) copy-start(pred[256]{0:T(512)(128)(4,1)} %get-tuple-element.87) | copy-start | bytes 772
  1011.5 13.1 collective-permute-start.17
  1013.1 13.3 collective-permute-start.15
  1021.1 10.8 collective-permute-start.16
  1021.1 12.4 collective-permute-start.18
  1024.6 9.8 collective-permute-start.19
  1039.3 411.5 %copy-start.13 = (f32[256,128]{0,1:T(8,128)}, f32[256,128]{0,1:T(8,128)S(1)}, u32[]{:S(2)}) copy-start(f32[256,128]{0,1:T(8,128)S(1)} %copy.287) | copy-start | bytes 393220
  1446.9 76.5 %copy-start.40 = (pred[256]{0:T(512)(128)(4,1)S(1)}, pred[256]{0:T(512)(128)(4,1)}, u32[]{:S(2)}) copy-start(pred[256]{0:T(512)(128)(4,1)} %compare_and_fusion.5) | copy-start | bytes 772
  1448.0 81.5 %copy-start.37 = (pred[256]{0:T(512)(128)(4,1)S(1)}, pred[256]{0:T(512)(128)(4,1)}, u32[]{:S(2)}) copy-start(pred[256]{0:T(512)(128)(4,1)} %compare_and_fusion.3) | copy-start | bytes 772
  1448.0 84.7 %copy-start.34 = (pred[256]{0:T(512)(128)(4,1)S(1)}, pred[256]{0:T(512)(128)(4,1)}, u32[]{:S(2)}) copy-start(pred[256]{0:T(512)(128)(4,1)} %compare_and_fusion) | copy-start | bytes 772
  1456.7 63.8 %collective-permute-start.22 = (f32[256,128]{0,1:T(8,128)}, f32[256,128]{0,1:T(8,128)S(1)}, u32[]{:S(2)}, u32[]{:S(2)}) collective-permute-start(f32[256,128]{0,1:T(8,128)} %get-tuple-element.41), channel_id=1, source_target_pairs={{64,0},{128,64},{192,128},{0,192},{65,1},{129,65},{193,129},{1,193... | collective-permute-start | bytes 393224 | tf_op jit(solution)/shard_map/ppermute | solution.py:23
  1512.7 8.7 collective-permute-start.20
  1516.3 11.6 collective-permute-start.21
  1517.8 12.4 collective-permute-start.23
  1520.1 11.7 collective-permute-start.24
  1549.0 30.8 %copy-start.11 = (f32[256,128]{0,1:T(8,128)S(1)}, f32[256,128]{0,1:T(8,128)}, u32[]{:S(2)}) copy-start(f32[256,128]{0,1:T(8,128)} %copy-done.10) | copy-start | bytes 393220
  1555.6 117.7 %copy-start.9 = (f32[256,128]{0,1:T(8,128)S(1)}, f32[256,128]{0,1:T(8,128)}, u32[]{:S(2)}) copy-start(f32[256,128]{0,1:T(8,128)} %copy-done.8) | copy-start | bytes 393220
  1555.6 12.7 collective-permute-start.25
  1560.4 118.3 %copy-start.7 = (f32[1,1,6,256,128]{3,4,2,1,0:T(8,128)S(1)}, f32[1,1,6,256,128]{3,4,2,1,0:T(8,128)}, u32[]{:S(2)}) copy-start(f32[1,1,6,256,128]{3,4,2,1,0:T(8,128)} %copy.254) | copy-start | bytes 2359300
  1560.4 17.8 %collective-permute-start.26 = (f32[256,128]{0,1:T(8,128)}, f32[256,128]{0,1:T(8,128)}, u32[]{:S(2)}, u32[]{:S(2)}) collective-permute-start(f32[256,128]{0,1:T(8,128)} %broadcast_select_fusion.1), channel_id=1, source_target_pairs={{0,1},{1,2},{2,3},{3,4},{4,5},{5,6},{6,7},{7,8},{8,9},{9,10},{10,1... | collective-permute-start | bytes 393224 | tf_op jit(solution)/shard_map/ppermute | solution.py:21
  1560.5 23.9 %collective-permute-start.28 = (f32[256,128]{0,1:T(8,128)}, f32[256,128]{0,1:T(8,128)}, u32[]{:S(2)}, u32[]{:S(2)}) collective-permute-start(f32[256,128]{0,1:T(8,128)} %broadcast_select_fusion), channel_id=1, source_target_pairs={{0,64},{64,128},{128,192},{192,0},{1,65},{65,129},{129,193},{193,1... | collective-permute-start | bytes 393224 | tf_op jit(solution)/shard_map/ppermute | solution.py:21
  1564.2 9.1 collective-permute-start.27
  1565.9 24.8 %collective-permute-start.29 = (f32[2,256,128]{1,2,0:T(8,128)}, f32[2,256,128]{1,2,0:T(8,128)}, u32[]{:S(2)}, u32[]{:S(2)}) collective-permute-start(f32[2,256,128]{1,2,0:T(8,128)} %pad_maximum_fusion.5), channel_id=1, source_target_pairs={{0,32},{1,33},{2,34},{3,35},{4,36},{5,37},{6,38},{7,39},{8,40},{9,... | collective-permute-start | bytes 786440 | tf_op jit(solution)/shard_map/ppermute | solution.py:31
  1568.3 109.8 %copy-start.17 = (f32[2,256,128]{1,2,0:T(8,128)S(1)}, f32[2,256,128]{1,2,0:T(8,128)}, u32[]{:S(2)}) copy-start(f32[2,256,128]{1,2,0:T(8,128)} %copy-done.16) | copy-start | bytes 786436
  (11 other events, 19.7 us)
Sparse Core Ops, SparseCore 0:
  10.9 2.5 sort.21.cloned.1.call-done
  (1 shorter events, 0.0 us)
where the time goes:
time: 1700 us; the launch traced here: 1690 us
  blocking collectives  1190 us (70%)
  starting transfers between devices  212 us (12%)
  local copies, waits for them, and re-layouts  131 us (8%)
  other arithmetic  76 us (4%)
  matrix products  45.8 us (3%)
  waiting for transfers between devices  20.2 us (1%)
    psum x3, blocking collectives, per_device(): gathered = lax.psum(selector[:, None, None] * projected[None], 'sub')  959 us
    psum x3, blocking collectives, per_device(): lax.psum((jnp.sum(residual * search, axis=(0, 1)), jnp.sum(search * assem...  231 us
    ppermute x12, starting transfers between devices, with_halo(): lax.ppermute(head, axis, [((i + 1) % count, i) for i in range(count)])  140 us
    ppermute x12, starting transfers between devices, with_halo(): lax.ppermute(tail, axis, [(i, (i + 1) % count) for i in range(count)])  70.9 us
    dot_general x3, matrix products, per_device(): jnp.dot(operator, local_copy.reshape(ORDER, COLS), precision=highest)  36.7 us
  transfers between devices with their start and end apart: 30, of which 6 were waited for; matrix products, arithmetic and copies ran while one was open for 5% of the time, Pallas kernels for 0%

commit v1 on v0

--- a/solution.py
+++ b/solution.py
@@ -96,8 +96,11 @@
         )
         assembled = owned * (applied - partner_values(applied, pairing, inverse))
         numerator, denominator = lax.psum(
-            (jnp.sum(residual * search, axis=(0, 1)), jnp.sum(search * assembled, axis=(0, 1))),
-            ("clus", "sub"),
+            lax.psum(
+                (jnp.sum(residual * search, axis=(0, 1)), jnp.sum(search * assembled, axis=(0, 1))),
+                "sub",
+            ),
+            "clus",
         )
         step_size = damping_factor * numerator / denominator
         multipliers = multipliers + step_size * search

time: 1700 us -> 2060 us (1.21)
  blocking collectives: 1190 us -> 1560 us
    psum x3, blocking collectives: 231 us -> 497 us  [per_device(): lax.psum((jnp.sum(residual * search, axis=(0, 1)), jnp.sum(search * assem...]
    psum x0 -> x3, blocking collectives: none -> 102 us  [per_device(): lax.psum(lax.psum((jnp.sum(residual * search, axis=(0, 1)), jnp.sum(searc...]
  transfers between devices with their start and end apart: 30 -> 30, of which waited for: 6 -> 5; matrix products, arithmetic and copies ran while one was open for 5% -> 4% of each run, Pallas kernels for 0% -> 0%
where the time goes in v1:
time: 2060 us
  blocking collectives  1560 us (76%)
  starting transfers between devices  205 us (10%)
  local copies, waits for them, and re-layouts  132 us (6%)
  other arithmetic  76.2 us (4%)
  matrix products  45.8 us (2%)
  waiting for transfers between devices  24.8 us (1%)
    psum x3, blocking collectives, per_device(): gathered = lax.psum(selector[:, None, None] * projected[None], 'sub')  957 us
    psum x3, blocking collectives, per_device(): lax.psum((jnp.sum(residual * search, axis=(0, 1)), jnp.sum(search * assem...  497 us
    ppermute x12, starting transfers between devices, with_halo(): lax.ppermute(head, axis, [((i + 1) % count, i) for i in range(count)])  138 us
    psum x3, blocking collectives, per_device(): lax.psum(lax.psum((jnp.sum(residual * search, axis=(0, 1)), jnp.sum(searc...  102 us
    ppermute x12, starting transfers between devices, with_halo(): lax.ppermute(tail, axis, [(i, (i + 1) % count) for i in range(count)])  65.9 us
  transfers between devices with their start and end apart: 30, of which 5 were waited for; matrix products, arithmetic and copies ran while one was open for 4% of the time, Pallas kernels for 0%

profile of v1, /device:TPU:1, one launch (start us, length us, event | category | flops | bytes accessed | tf_op | source)
XLA Modules:
  0.0 2056.1 jit_solution(11117957307006593966)
XLA Ops:
  22.3 326.6 %all-reduce.3 = (f32[2,32,128]{2,1,0:T(8,128)S(1)}, f32[2,32,32]{1,2,0:T(8,128)S(1)}) all-reduce(f32[2,32,128]{2,1,0:T(8,128)S(1)} %broadcast_multiply_fusion.3, f32[2,32,32]{1,2,0:T(8,128)S(1)} %broadcast_multiply_fusion.4), channel_id=1, replica_groups=mesh['clus'=4,'sub'=64] {'sub'}, use_global_device_ids=true, to_apply=%region_3.4 | all-reduce | flops 10240 | bytes 81920 | tf_op jit(solution)/shard_map/psum | solution.py:86
  349.0 5.9 custom-call.9
  355.1 4.9 custom-call.12
  360.5 1.8 convolution_bitcast_fusion.2
  363.7 2.1 multiply_subtract_fusion.9
  367.0 1.9 slice_bitcast_fusion.19
  373.3 56.8 %collective-permute-start.3 = (f32[256,128]{0,1:T(8,128)}, f32[256,128]{0,1:T(8,128)}, u32[]{:S(2)}, u32[]{:S(2)}) collective-permute-start(f32[256,128]{0,1:T(8,128)} %broadcast_select_fusion.10), channel_id=1, source_target_pairs={{0,64},{64,128},{128,192},{192,0},{1,65},{65,129},{129,193},{193,1... | collective-permute-start | bytes 393224 | tf_op jit(solution)/shard_map/ppermute | solution.py:21
  430.1 8.1 collective-permute-start
  439.5 3.8 collective-permute-done
  445.8 1.6 bitcast_dynamic-update-slice_fusion.46
  448.1 1.6 bitcast_dynamic-update-slice_fusion.44
  454.5 12.2 fusion.6
  472.0 8.7 collective-permute-start.5
  487.9 7.3 collective-permute-done.6
  497.9 1.6 multiply_reduce_fusion.5
  500.7 166.0 %all-reduce.2 = (f32[128]{0:T(128)S(1)}, f32[128]{0:T(128)S(1)}) all-reduce(f32[128]{0:T(128)S(1)} %get-tuple-element.13, f32[128]{0:T(128)S(1)} %get-tuple-element.12), channel_id=1, replica_groups=mesh['clus'=4,'sub'=64] {'sub'}, use_global_device_ids=true, to_apply=%region_9.12 | all-reduce | flops 256 | bytes 2048 | tf_op jit(solution)/shard_map/psum | solution.py:99
  666.7 33.7 %all-reduce.6 = (f32[128]{0:T(128)S(1)}, f32[128]{0:T(128)S(1)}) all-reduce(f32[128]{0:T(128)S(1)} %get-tuple-element.22, f32[128]{0:T(128)S(1)} %get-tuple-element.23), channel_id=1, replica_groups=mesh['clus'=4,'sub'=64] {'clus'}, use_global_device_ids=true, to_apply=%region_10.13 | all-reduce | flops 256 | bytes 2048 | tf_op jit(solution)/shard_map/psum | solution.py:98
  704.1 315.0 %psum.118 = f32[2,32,128]{2,1,0:T(8,128)S(1)} all-reduce(f32[2,32,128]{2,1,0:T(8,128)S(1)} %broadcast_multiply_fusion.2), channel_id=1, replica_groups=mesh['clus'=4,'sub'=64] {'sub'}, use_global_device_ids=true, to_apply=%region_11.14 | all-reduce | flops 8192 | bytes 65536 | tf_op jit(solution)/shard_map/psum | solution.py:86
  1021.5 2.3 copy.260
  1023.8 2.6 multiply_subtract_fusion.6
  1034.7 56.1 %collective-permute-start.12 = (f32[256,128]{0,1:T(8,128)}, f32[256,128]{0,1:T(8,128)S(1)}, u32[]{:S(2)}, u32[]{:S(2)}) collective-permute-start(f32[256,128]{0,1:T(8,128)} %get-tuple-element.59), channel_id=1, source_target_pairs={{64,0},{128,64},{192,128},{0,192},{65,1},{129,65},{193,129},{1,193... | collective-permute-start | bytes 393224 | tf_op jit(solution)/shard_map/ppermute | solution.py:23
  1092.1 2.3 copy.292
  1096.3 1.6 pad_maximum_fusion.2
  1101.6 4.5 collective-permute-done.11
  1111.4 1.6 slice_dynamic-update-slice_fusion.1
  1115.5 12.1 fusion.9
  1133.0 1.6 collective-permute-start.17
  1134.6 4.4 collective-permute-start.15
  1143.0 1.6 pad_maximum_fusion.3
  1150.0 3.3 collective-permute-done.16
  1155.7 1.6 slice_bitcast_fusion.8
  1163.4 2.3 copy.294
  1165.7 1.9 multiply_reduce_fusion.3
  1167.5 165.9 %all-reduce.1 = (f32[128]{0:T(128)S(1)}, f32[128]{0:T(128)}) all-reduce(f32[128]{0:T(128)S(1)} %get-tuple-element.17, f32[128]{0:T(128)S(1)} %get-tuple-element.16), channel_id=1, replica_groups=mesh['clus'=4,'sub'=64] {'sub'}, use_global_device_ids=true, to_apply=%region_16.19 | all-reduce | flops 256 | bytes 2048 | tf_op jit(solution)/shard_map/psum | solution.py:99
  1333.4 33.9 %all-reduce.5 = (f32[128]{0:T(128)S(1)}, f32[128]{0:T(128)S(1)}) all-reduce(f32[128]{0:T(128)S(1)} %get-tuple-element.20, f32[128]{0:T(128)} %get-tuple-element.21), channel_id=1, replica_groups=mesh['clus'=4,'sub'=64] {'clus'}, use_global_device_ids=true, to_apply=%region_17.20 | all-reduce | flops 256 | bytes 2048 | tf_op jit(solution)/shard_map/psum | solution.py:98
  1371.6 315.2 %psum.123 = f32[2,32,128]{2,1,0:T(8,128)S(1)} all-reduce(f32[2,32,128]{2,1,0:T(8,128)S(1)} %broadcast_multiply_fusion.1), channel_id=1, replica_groups=mesh['clus'=4,'sub'=64] {'sub'}, use_global_device_ids=true, to_apply=%region_18.21 | all-reduce | flops 8192 | bytes 65536 | tf_op jit(solution)/shard_map/psum | solution.py:86
  1690.4 2.8 multiply_subtract_fusion.2
  1699.1 55.9 %collective-permute-start.22 = (f32[256,128]{0,1:T(8,128)}, f32[256,128]{0,1:T(8,128)S(1)}, u32[]{:S(2)}, u32[]{:S(2)}) collective-permute-start(f32[256,128]{0,1:T(8,128)} %get-tuple-element.47), channel_id=1, source_target_pairs={{64,0},{128,64},{192,128},{0,192},{65,1},{129,65},{193,129},{1,193... | collective-permute-start | bytes 393224 | tf_op jit(solution)/shard_map/ppermute | solution.py:23
  1756.3 2.3 copy.329
  1764.4 5.8 collective-permute-done.21
  1770.2 1.6 bitcast_dynamic-update-slice_fusion.20
  1772.5 1.6 bitcast_dynamic-update-slice_fusion.18
  1778.9 12.4 fusion.12
  1797.9 1.8 collective-permute-start.25
  1801.4 3.8 collective-permute-start.28
  1805.2 1.7 pad_maximum_fusion.5
  1811.3 1.8 bitcast_dynamic-update-slice_fusion.5
  1816.1 1.6 bitcast_dynamic-update-slice_fusion.10
  1817.7 1.6 bitcast_dynamic-update-slice_fusion.26
  1819.3 1.6 bitcast_dynamic-update-slice_fusion.4
  1820.9 1.7 bitcast_dynamic-update-slice_fusion.3
  1822.6 1.6 bitcast_dynamic-update-slice_fusion.15
  1825.4 1.6 bitcast_dynamic-update-slice_fusion.13
  1827.0 1.6 bitcast_dynamic-update-slice_fusion.2
  1828.6 1.6 bitcast_dynamic-update-slice_fusion.8
  1830.1 1.6 bitcast_dynamic-update-slice_fusion.24
  1834.9 1.6 slice_dynamic-update-slice_fusion.3
  1836.4 1.9 multiply_reduce_fusion.1
  1838.3 164.8 %all-reduce = (f32[128]{0:T(128)S(1)}, f32[128]{0:T(128)S(1)}) all-reduce(f32[128]{0:T(128)S(1)} %get-tuple-element.15, f32[128]{0:T(128)S(1)} %get-tuple-element.14), channel_id=1, replica_groups=mesh['clus'=4,'sub'=64] {'sub'}, use_global_device_ids=true, to_apply=%region_23.26 | all-reduce | flops 256 | bytes 2048 | tf_op jit(solution)/shard_map/psum | solution.py:99
  2003.1 34.2 %all-reduce.4 = (f32[128]{0:T(128)S(1)}, f32[128]{0:T(128)S(1)}) all-reduce(f32[128]{0:T(128)S(1)} %get-tuple-element.18, f32[128]{0:T(128)S(1)} %get-tuple-element.19), channel_id=1, replica_groups=mesh['clus'=4,'sub'=64] {'clus'}, use_global_device_ids=true, to_apply=%region_24.27 | all-reduce | flops 256 | bytes 2048 | tf_op jit(solution)/shard_map/psum | solution.py:98
  2037.3 1.7 bitcast_dynamic-update-slice_fusion.1
  2039.0 1.6 bitcast_dynamic-update-slice_fusion
  2040.6 1.6 bitcast_dynamic-update-slice_fusion.6
  2042.8 3.7 multiply_subtract_fusion
  (390 shorter events, 148.3 us)
Async XLA Ops:
  12.8 473.6 %copy-start.20 = (s32[1024]{0:T(1024)}, s32[1024]{0:T(1024)S(1)}, u32[]{:S(2)}) copy-start(s32[1024]{0:T(1024)S(1)} %pad_clamp_fusion.5) | copy-start | bytes 12292
  12.8 347.4 %copy-start.41 = (f32[2]{0:T(128)}, f32[2]{0:T(128)S(1)}, u32[]{:S(2)}) copy-start(f32[2]{0:T(128)S(1)} %compare_convert_fusion) | copy-start | bytes 28
  15.7 438.8 %copy-start.1 = (f32[1536,128]{0,1:T(8,128)}, f32[1536,128]{0,1:T(8,128)S(1)}, u32[]{:S(2)}) copy-start(f32[1536,128]{0,1:T(8,128)S(1)} %copy.224) | copy-start | bytes 2359300
  18.3 451.4 %copy-start.22 = (s32[1024]{0:T(1024)}, s32[1024]{0:T(1024)S(1)}, u32[]{:S(2)}) copy-start(s32[1024]{0:T(1024)S(1)} %pad_clamp_fusion.4) | copy-start | bytes 12292
  19.3 352.7 %copy-start.23 = (pred[256]{0:T(512)(128)(4,1)S(1)}, pred[256]{0:T(512)(128)(4,1)}, u32[]{:S(2)}) copy-start(pred[256]{0:T(512)(128)(4,1)} %get-tuple-element.93) | copy-start | bytes 772
  19.3 353.4 %copy-start.26 = (pred[256]{0:T(512)(128)(4,1)S(1)}, pred[256]{0:T(512)(128)(4,1)}, u32[]{:S(2)}) copy-start(pred[256]{0:T(512)(128)(4,1)} %get-tuple-element.92) | copy-start | bytes 772
  19.3 418.9 %copy-start.29 = (pred[256]{0:T(512)(128)(4,1)S(1)}, pred[256]{0:T(512)(128)(4,1)}, u32[]{:S(2)}) copy-start(pred[256]{0:T(512)(128)(4,1)} %get-tuple-element.91) | copy-start | bytes 772
  362.2 82.9 %copy-start.38 = (pred[256]{0:T(512)(128)(4,1)S(1)}, pred[256]{0:T(512)(128)(4,1)}, u32[]{:S(2)}) copy-start(pred[256]{0:T(512)(128)(4,1)} %compare_and_fusion.5) | copy-start | bytes 772
  362.2 85.2 %copy-start.35 = (pred[256]{0:T(512)(128)(4,1)S(1)}, pred[256]{0:T(512)(128)(4,1)}, u32[]{:S(2)}) copy-start(pred[256]{0:T(512)(128)(4,1)} %compare_and_fusion.3) | copy-start | bytes 772
  363.7 86.9 %copy-start.32 = (pred[256]{0:T(512)(128)(4,1)S(1)}, pred[256]{0:T(512)(128)(4,1)}, u32[]{:S(2)}) copy-start(pred[256]{0:T(512)(128)(4,1)} %compare_and_fusion) | copy-start | bytes 772
  372.6 73.2 %collective-permute-start.1 = (f32[256,128]{0,1:T(8,128)}, f32[256,128]{0,1:T(8,128)}, u32[]{:S(2)}, u32[]{:S(2)}) collective-permute-start(f32[256,128]{0,1:T(8,128)} %broadcast_select_fusion.11), channel_id=1, source_target_pairs={{0,1},{1,2},{2,3},{3,4},{4,5},{5,6},{6,7},{7,8},{8,9},{9,10},{10,1... | collective-permute-start | bytes 393224 | tf_op jit(solution)/shard_map/ppermute | solution.py:21
  373.3 74.8 %collective-permute-start.3 = (f32[256,128]{0,1:T(8,128)}, f32[256,128]{0,1:T(8,128)}, u32[]{:S(2)}, u32[]{:S(2)}) collective-permute-start(f32[256,128]{0,1:T(8,128)} %broadcast_select_fusion.10), channel_id=1, source_target_pairs={{0,64},{64,128},{128,192},{192,0},{1,65},{65,129},{129,193},{193,1... | collective-permute-start | bytes 393224 | tf_op jit(solution)/shard_map/ppermute | solution.py:21
  430.1 8.4 collective-permute-start.2
  430.1 13.2 collective-permute-start
  438.2 11.4 collective-permute-start.4
  451.9 15.9 copy-start.30
  453.3 15.6 copy-start.27
  454.5 26.3 %copy-start.24 = (pred[256]{0:T(512)(128)(4,1)S(1)}, pred[256]{0:T(512)(128)(4,1)}, u32[]{:S(2)}) copy-start(pred[256]{0:T(512)(128)(4,1)} %get-tuple-element.93) | copy-start | bytes 772
  470.5 14.9 collective-permute-start.7
  472.0 14.3 collective-permute-start.5
  482.9 219.7 %copy-start = (f32[1,1,32,1536]{3,2,1,0:T(8,128)S(1)}, f32[1,1,32,1536]{3,2,1,0:T(8,128)}, u32[]{:S(2)}) copy-start(f32[1,1,32,1536]{3,2,1,0:T(8,128)} %param.11) | copy-start | bytes 589828
  484.0 11.3 collective-permute-start.6
  484.0 11.9 collective-permute-start.8
  485.4 10.6 collective-permute-start.9
  486.3 9.8 copy-start.10
  487.3 8.7 copy-start.12
  496.9 529.5 %copy-start.8 = (f32[256,128]{0,1:T(8,128)}, f32[256,128]{0,1:T(8,128)S(1)}, u32[]{:S(2)}) copy-start(f32[256,128]{0,1:T(8,128)S(1)} %copy.251) | copy-start | bytes 393220
  1020.4 78.8 %copy-start.21 = (s32[1024]{0:T(1024)S(1)}, s32[1024]{0:T(1024)}, u32[]{:S(2)}) copy-start(s32[1024]{0:T(1024)} %copy-done.20) | copy-start | bytes 12292
  1021.5 79.1 %copy-start.39 = (pred[256]{0:T(512)(128)(4,1)S(1)}, pred[256]{0:T(512)(128)(4,1)}, u32[]{:S(2)}) copy-start(pred[256]{0:T(512)(128)(4,1)} %compare_and_fusion.5) | copy-start | bytes 772
  1023.8 83.1 %copy-start.36 = (pred[256]{0:T(512)(128)(4,1)S(1)}, pred[256]{0:T(512)(128)(4,1)}, u32[]{:S(2)}) copy-start(pred[256]{0:T(512)(128)(4,1)} %compare_and_fusion.3) | copy-start | bytes 772
  1023.8 86.8 %copy-start.33 = (pred[256]{0:T(512)(128)(4,1)S(1)}, pred[256]{0:T(512)(128)(4,1)}, u32[]{:S(2)}) copy-start(pred[256]{0:T(512)(128)(4,1)} %compare_and_fusion) | copy-start | bytes 772
  1027.6 87.9 %copy-start.4 = (f32[1536,128]{0,1:T(8,128)S(1)}, f32[1536,128]{0,1:T(8,128)}, u32[]{:S(2)}) copy-start(f32[1536,128]{0,1:T(8,128)} %copy-done.3) | copy-start | bytes 2359300
  1034.7 63.5 %collective-permute-start.12 = (f32[256,128]{0,1:T(8,128)}, f32[256,128]{0,1:T(8,128)S(1)}, u32[]{:S(2)}, u32[]{:S(2)}) collective-permute-start(f32[256,128]{0,1:T(8,128)} %get-tuple-element.59), channel_id=1, source_target_pairs={{64,0},{128,64},{192,128},{0,192},{65,1},{129,65},{193,129},{1,193... | collective-permute-start | bytes 393224 | tf_op jit(solution)/shard_map/ppermute | solution.py:23
  1090.8 8.3 collective-permute-start.10
  1094.4 11.6 collective-permute-start.11
  1095.9 11.1 collective-permute-start.13
  1098.0 10.0 collective-permute-start.14
  1112.9 16.6 copy-start.31
  1114.3 16.9 copy-start.28
  1115.5 23.5 %copy-start.25 = (pred[256]{0:T(512)(128)(4,1)S(1)}, pred[256]{0:T(512)(128)(4,1)}, u32[]{:S(2)}) copy-start(pred[256]{0:T(512)(128)(4,1)} %get-tuple-element.93) | copy-start | bytes 772
  1133.0 11.7 collective-permute-start.17
  1134.6 11.9 collective-permute-start.15
  1142.2 11.1 collective-permute-start.16
  1142.2 12.6 collective-permute-start.18
  1144.6 11.1 collective-permute-start.19
  1146.5 9.2 copy-start.14
  1160.7 532.5 %copy-start.13 = (f32[256,128]{0,1:T(8,128)}, f32[256,128]{0,1:T(8,128)S(1)}, u32[]{:S(2)}) copy-start(f32[256,128]{0,1:T(8,128)S(1)} %copy.287) | copy-start | bytes 393220
  1689.2 74.5 %copy-start.40 = (pred[256]{0:T(512)(128)(4,1)S(1)}, pred[256]{0:T(512)(128)(4,1)}, u32[]{:S(2)}) copy-start(pred[256]{0:T(512)(128)(4,1)} %compare_and_fusion.5) | copy-start | bytes 772
  1690.4 81.5 %copy-start.37 = (pred[256]{0:T(512)(128)(4,1)S(1)}, pred[256]{0:T(512)(128)(4,1)}, u32[]{:S(2)}) copy-start(pred[256]{0:T(512)(128)(4,1)} %compare_and_fusion.3) | copy-start | bytes 772
  1690.4 84.6 %copy-start.34 = (pred[256]{0:T(512)(128)(4,1)S(1)}, pred[256]{0:T(512)(128)(4,1)}, u32[]{:S(2)}) copy-start(pred[256]{0:T(512)(128)(4,1)} %compare_and_fusion) | copy-start | bytes 772
  1699.1 61.8 %collective-permute-start.22 = (f32[256,128]{0,1:T(8,128)}, f32[256,128]{0,1:T(8,128)S(1)}, u32[]{:S(2)}, u32[]{:S(2)}) collective-permute-start(f32[256,128]{0,1:T(8,128)} %get-tuple-element.47), channel_id=1, source_target_pairs={{64,0},{128,64},{192,128},{0,192},{65,1},{129,65},{193,129},{1,193... | collective-permute-start | bytes 393224 | tf_op jit(solution)/shard_map/ppermute | solution.py:23
  1755.0 6.8 collective-permute-start.20
  1758.6 11.6 collective-permute-start.21
  1760.1 12.4 collective-permute-start.23
  1760.5 13.6 collective-permute-start.24
  1791.3 29.6 %copy-start.11 = (f32[256,128]{0,1:T(8,128)S(1)}, f32[256,128]{0,1:T(8,128)}, u32[]{:S(2)}) copy-start(f32[256,128]{0,1:T(8,128)} %copy-done.10) | copy-start | bytes 393220
  1797.9 239.4 %copy-start.9 = (f32[256,128]{0,1:T(8,128)S(1)}, f32[256,128]{0,1:T(8,128)}, u32[]{:S(2)}) copy-start(f32[256,128]{0,1:T(8,128)} %copy-done.8) | copy-start | bytes 393220
  1797.9 11.3 collective-permute-start.25
  1801.3 241.5 %copy-start.7 = (f32[1,1,6,256,128]{3,4,2,1,0:T(8,128)S(1)}, f32[1,1,6,256,128]{3,4,2,1,0:T(8,128)}, u32[]{:S(2)}) copy-start(f32[1,1,6,256,128]{3,4,2,1,0:T(8,128)} %copy.254) | copy-start | bytes 2359300
  1801.4 17.9 collective-permute-start.26
  1801.4 24.0 %collective-permute-start.28 = (f32[256,128]{0,1:T(8,128)}, f32[256,128]{0,1:T(8,128)}, u32[]{:S(2)}, u32[]{:S(2)}) collective-permute-start(f32[256,128]{0,1:T(8,128)} %broadcast_select_fusion), channel_id=1, source_target_pairs={{0,64},{64,128},{128,192},{192,0},{1,65},{65,129},{129,193},{193,1... | collective-permute-start | bytes 393224 | tf_op jit(solution)/shard_map/ppermute | solution.py:21
  1805.2 9.1 collective-permute-start.27
  1806.9 24.8 %collective-permute-start.29 = (f32[2,256,128]{1,2,0:T(8,128)}, f32[2,256,128]{1,2,0:T(8,128)}, u32[]{:S(2)}, u32[]{:S(2)}) collective-permute-start(f32[2,256,128]{1,2,0:T(8,128)} %pad_maximum_fusion.5), channel_id=1, source_target_pairs={{0,32},{1,33},{2,34},{3,35},{4,36},{5,37},{6,38},{7,39},{8,40},{9,... | collective-permute-start | bytes 786440 | tf_op jit(solution)/shard_map/ppermute | solution.py:31
  1809.2 232.9 %copy-start.17 = (f32[2,256,128]{1,2,0:T(8,128)S(1)}, f32[2,256,128]{1,2,0:T(8,128)}, u32[]{:S(2)}) copy-start(f32[2,256,128]{1,2,0:T(8,128)} %copy-done.16) | copy-start | bytes 786436
  (11 other events, 20.2 us)
Sparse Core Ops, SparseCore 0:
  10.9 2.5 sort.21.cloned.1.call-done
  (1 shorter events, 0.0 us)
